TPU v7x, 32 devices: a whole 2x2x4 slice. The times are simulated.
32 devices in a mesh: tm: 4 (over z), feat: 8 (over y, x, core).
Axes of the slice: x: 2, y: 2, z: 4, core: 2. Of those that a mesh axis runs over, the one named last changes fastest.
Arguments:
- trajectory: float32 [16384, 2048], P('tm', 'feat'), may hold values from -8 to 9
Outputs:
- moments: float32 [4, 2048, 2048], P(None, 'feat', 'tm')
All inputs are finite; a program needn't handle non-finite values.
Results may differ from a plain program's by a relative error of at most 0.00035.
Values may be sent and summed in bfloat16 or wider, within the bound.
No kernel may reach another device: no remote copies, remote signals or barrier semaphores. Data moves between devices by JAX's collectives and lax.ppermute only.
A program may use at most 128 MiB of HBM per device.

v0:
```python
import jax
import jax.numpy as jnp
from jax import lax
from jax.sharding import PartitionSpec as P

HALO = 16
lag_values = (0, 1, 4, 16)


def passed_along(value, axis, steps):
    count = lax.axis_size(axis)
    initial, last = (max(0, -steps), min(count, count - steps))
    return lax.ppermute(value, axis, [(source, source + steps) for source in range(initial, last)])


def shards(trajectory):
    rows = trajectory.shape[0]
    frames = rows * lax.axis_size("tm")
    total = lax.psum(jnp.sum(trajectory, axis=0), "tm")
    mean = total / frames
    centered = (trajectory - mean).astype(jnp.bfloat16)
    gathered = lax.all_gather(centered, "feat", axis=1, tiled=True)
    tail = passed_along(gathered[:HALO], "tm", -1)
    extended = jnp.concatenate([gathered, tail], axis=0)
    blocks = [
        lax.dot_general(
            centered,
            extended[lag : lag + rows],
            (((0,), (0,)), ((), ())),
            preferred_element_type=jnp.float32,
        )
        for lag in lag_values
    ]
    partial_sum = jnp.stack(blocks)
    summed = lax.psum_scatter(partial_sum, "tm", scatter_dimension=2, tiled=True)
    scales = jnp.sqrt(jnp.float32(frames) - jnp.array(lag_values, jnp.float32))
    return summed / scales[:, None, None]


def solution(mesh):
    placed = (P("tm", "feat"),)
    return jax.shard_map(
        shards, mesh=mesh, in_specs=placed, out_specs=P(None, "feat", "tm"), check_vma=False
    )
```

profile of v0, /device:TPU:0, one launch (start us, length us, event | category | flops | bytes accessed | tf_op | source)
XLA Modules:
  0.0 323.2 jit_solution(11681123390294850944)
XLA Ops:
  6.5 0.0 all-gather.2.cloned.1.call-start
  6.5 2.7 reduce_sum.9
  9.3 13.5 %psum.7 = f32[256]{0:T(256)S(1)} all-reduce(f32[256]{0:T(256)S(1)} %reduce_sum.9), channel_id=1, replica_groups=mesh['tm'=4,'feat'=8] {'tm'}, use_global_device_ids=true, to_apply=%region_1.0 | all-reduce | flops 256 | bytes 2048 | tf_op jit(solution)/shard_map/psum | solution.py:19
  22.8 3.9 %subtract_convert_fusion = bf16[4096,256]{1,0:T(8,128)(2,1)} fusion(f32[4096,256]{1,0:T(8,128)} %param.2, f32[256]{0:T(256)S(1)} %broadcast_multiply_fusion.1), kind=kLoop, calls=%fused_computation.7 | loop fusion | flops 2097152 | bytes 6292480 | tf_op jit(solution)/shard_map/convert_element_type | solution.py:21
  26.6 0.0 all-gather.2.cloned.1.call-update
  26.7 0.0 reduce-scatter.2.cloned.1.call-start
  26.7 91.3 %all-gather.2.cloned.1.call-done = bf16[4096,2048]{1,0:T(8,128)(2,1)} async-done(((bf16[4096,256]{1,0:T(8,128)(2,1)}), bf16[4096,2048]{1,0:T(8,128)(2,1)}) %all-gather.2.cloned.1.call-update) | async-done | bytes 16777232 | tf_op jit(solution)/shard_map/all_gather | solution.py:22
  118.0 0.8 slice.16
  118.9 1.3 collective-permute-start
  120.2 0.0 copy-start
  120.2 8.9 %convolution_bitcast_fusion = f32[1,256,2048]{2,1,0:T(8,128)S(1)} fusion(bf16[4096,256]{1,0:T(8,128)(2,1)} %subtract_convert_fusion, bf16[4096,2048]{1,0:T(8,128)(2,1)} %all-gather.2.cloned.1.call-done), kind=kOutput, calls=%fused_computation.11 | convolution fusion | flops 4294967296 | bytes 20971520 | tf_op jit(solution)/shard_map/dot_general | solution.py:26
  129.1 2.2 copy-done
  131.3 0.0 copy-start.1
  131.3 7.0 %constant_dynamic-update-slice_fusion.1 = bf16[4112,2048]{1,0:T(8,128)(2,1)} fusion(bf16[4096,2048]{1,0:T(8,128)(2,1)S(1)} %copy-done), kind=kLoop, calls=%fused_computation.14 | loop fusion | bytes 33554432
  138.3 0.0 collective-permute-done
  138.3 0.6 constant_dynamic-update-slice_fusion
  138.9 0.0 copy-done.1
  138.9 8.2 %fusion.12 = f32[1,256,2048]{2,1,0:T(8,128)S(1)} fusion(bf16[4096,256]{1,0:T(8,128)(2,1)S(1)} %copy-done.1, bf16[4112,2048]{1,0:T(8,128)(2,1)} %constant_dynamic-update-slice_fusion), kind=kOutput, calls=%fused_computation.10 | convolution fusion | flops 4294967296 | bytes 20971520 | tf_op jit(solution)/shard_map/dot_general | solution.py:26
  147.1 8.2 %fusion.9 = f32[1,256,2048]{2,1,0:T(8,128)S(1)} fusion(bf16[4096,256]{1,0:T(8,128)(2,1)S(1)} %copy-done.1, bf16[4112,2048]{1,0:T(8,128)(2,1)} %constant_dynamic-update-slice_fusion), kind=kOutput, calls=%fused_computation.9 | convolution fusion | flops 4294967296 | bytes 20971520 | tf_op jit(solution)/shard_map/dot_general | solution.py:26
  155.3 8.2 %fusion.6 = f32[1,256,2048]{2,1,0:T(8,128)S(1)} fusion(bf16[4096,256]{1,0:T(8,128)(2,1)S(1)} %copy-done.1, bf16[4112,2048]{1,0:T(8,128)(2,1)} %constant_dynamic-update-slice_fusion), kind=kOutput, calls=%fused_computation.8 | convolution fusion | flops 4294967296 | bytes 20971520 | tf_op jit(solution)/shard_map/dot_general | solution.py:26
  163.5 3.7 %pad_maximum_fusion = f32[4,256,2048]{2,1,0:T(8,128)} fusion(f32[1,256,2048]{2,1,0:T(8,128)S(1)} %fusion.12, f32[1,256,2048]{2,1,0:T(8,128)S(1)} %fusion.9, f32[1,256,2048]{2,1,0:T(8,128)S(1)} %fusion.6, f32[1,256,2048]{2,1,0:T(8,128)S(1)} %convolution_bitcast_fusion), kind=kLoop, calls=%fused_computation.6 | loop fusion | flops 6291456 | bytes 16777216 | tf_op jit(solution)/shard_map/stack | solution.py:34
  167.2 0.0 copy-start.2
  167.2 0.0 reduce-scatter.2.cloned.1.call-update
  167.2 145.9 %reduce-scatter.2.cloned.1.call-done = f32[4,256,512]{2,1,0:T(8,128)} async-done(((f32[4,256,2048]{2,1,0:T(8,128)}), f32[4,256,512]{2,1,0:T(8,128)}) %reduce-scatter.2.cloned.1.call-update) | async-done | bytes 2097168 | tf_op jit(solution)/shard_map/reduce_scatter | solution.py:35
  313.1 0.0 copy-done.2
  313.1 3.3 %broadcast_multiply_fusion = f32[4,256,512]{2,1,0:T(8,128)} fusion(f32[4,256,512]{2,1,0:T(8,128)} %reduce-scatter.2.cloned.1.call-done, f32[4]{0:T(128)S(1)} %copy-done.2), kind=kLoop, calls=%fused_computation.12 | loop fusion | flops 524288 | bytes 4194320 | tf_op jit(solution)/shard_map/div | solution.py:37
  (1 shorter events, 0.0 us)
Async XLA Ops:
  6.5 111.5 %all-gather.2.cloned.1.call-start = ((), (), s32[]{:S(2)}) async-start(), calls=%async_computation.1 | async-start | bytes 18874368 | tf_op jit(solution)/shard_map/all_gather | solution.py:22
  26.7 286.4 %reduce-scatter.2.cloned.1.call-start = ((), (), s32[]{:S(2)}) async-start(), calls=%async_computation.2 | async-start | bytes 10485760 | tf_op jit(solution)/shard_map/reduce_scatter | solution.py:35
  118.9 19.4 %collective-permute-start = (bf16[16,2048]{1,0:T(8,128)(2,1)S(1)}, bf16[16,2048]{1,0:T(8,128)(2,1)S(1)}, u32[]{:S(2)}, u32[]{:S(2)}) collective-permute-start(bf16[16,2048]{1,0:T(8,128)(2,1)S(1)} %slice.16), channel_id=1, source_target_pairs={{8,0},{16,8},{24,16},{9,1},{17,9},{25,17},{10,2},{18,10},{26,18},{... | collective-permute-start | bytes 196616 | tf_op jit(solution)/shard_map/ppermute | solution.py:13
  120.2 11.1 %copy-start = (bf16[4096,2048]{1,0:T(8,128)(2,1)S(1)}, bf16[4096,2048]{1,0:T(8,128)(2,1)}, u32[]{:S(2)}) copy-start(bf16[4096,2048]{1,0:T(8,128)(2,1)} %all-gather.2.cloned.1.call-done) | copy-start | bytes 50331652
  131.3 7.6 %copy-start.1 = (bf16[4096,256]{1,0:T(8,128)(2,1)S(1)}, bf16[4096,256]{1,0:T(8,128)(2,1)}, u32[]{:S(2)}) copy-start(bf16[4096,256]{1,0:T(8,128)(2,1)} %subtract_convert_fusion) | copy-start | bytes 6291460
  167.2 145.9 %copy-start.2 = (f32[4]{0:T(128)S(1)}, f32[4]{0:T(128)}, u32[]{:S(2)}) copy-start(f32[4]{0:T(128)} %constant.13) | copy-start | bytes 52
Sparse Core Ops, SparseCore 0:
  26.8 91.2 all-gather.1
  167.3 145.7 reduce-scatter.1
where the time goes:
time: 324 us; the launch traced here: 323 us
  waiting for transfers between devices  237 us (73%)
  matrix products  33.5 us (10%)
  other arithmetic  13.5 us (4%)
  blocking collectives  13.5 us (4%)
  between operations  13.5 us (4%)
  local copies, waits for them, and re-layouts  10.7 us (3%)
    reduce_scatter x1, waiting for transfers between devices, shards(): lax.psum_scatter(partial_sum, 'tm', scatter_dimension=2, tiled=True)  146 us
    all_gather x1, waiting for transfers between devices, shards(): gathered = lax.all_gather(centered, 'feat', axis=1, tiled=True)  91.3 us
    dot_general x4, matrix products, shards(): lax.dot_general(centered, extended[lag:lag + rows], (((0,), (0,)), ((), (...  33.5 us
    psum x1, blocking collectives, shards(): total = lax.psum(jnp.sum(trajectory, axis=0), 'tm')  13.5 us
    unnamed x7, local copies, waits for them, and re-layouts  9.21 us
  transfers between devices with their start and end apart: 3, of which 2 were waited for; matrix products, arithmetic and copies ran while one was open for 5% of the time, Pallas kernels for 0%

commit v1 on v0

--- a/solution.py
+++ b/solution.py
@@ -1,3 +1,4 @@
+import functools
 import jax
 import jax.numpy as jnp
 from jax import lax
@@ -5,6 +6,24 @@
 
 HALO = 16
 lag_values = (0, 1, 4, 16)
+
+
+def match_the_spots(tile_in, group_axis, on_dim):
+    n = lax.axis_size(group_axis)
+    state_next = sorted(((src_i, (src_i + 1) % n) for src_i in range(n)))
+    clean = tile_in
+    ledger = [clean]
+    for rr in [*range(1, n)]:
+        clean = lax.ppermute(clean, axis_name=group_axis, perm=state_next)
+        ledger.insert(0, clean)
+    return jnp.roll(
+        jnp.concatenate(ledger, axis=on_dim),
+        (lax.axis_index(group_axis) + 1) * tile_in.shape[on_dim],
+        axis=on_dim,
+    )
+
+
+note_the_hubs = functools.partial(match_the_spots, group_axis="feat", on_dim=1)
 
 
 def passed_along(value, axis, steps):
@@ -19,7 +38,7 @@
     total = lax.psum(jnp.sum(trajectory, axis=0), "tm")
     mean = total / frames
     centered = (trajectory - mean).astype(jnp.bfloat16)
-    gathered = lax.all_gather(centered, "feat", axis=1, tiled=True)
+    gathered = note_the_hubs(centered)
     tail = passed_along(gathered[:HALO], "tm", -1)
     extended = jnp.concatenate([gathered, tail], axis=0)
     blocks = [

time: 324 us -> 455 us (1.40)
  waiting for transfers between devices: 237 us -> 327 us
  local copies, waits for them, and re-layouts: 10.7 us -> 49.8 us
    ppermute x0 -> x7, waiting for transfers between devices: none -> 185 us  [match_the_spots(): clean = lax.ppermute(clean, axis_name=group_axis, perm=state_next)]
    all_gather x1 -> x0, waiting for transfers between devices: 91.3 us -> none  [shards(): gathered = lax.all_gather(centered, 'feat', axis=1, tiled=True)]
    unnamed x7 -> x40, local copies, waits for them, and re-layouts: 9.21 us -> 40.4 us
    dynamic_slice x0 -> x1, local copies, waits for them, and re-layouts: none -> 8.48 us  [match_the_spots(): jnp.roll(jnp.concatenate(ledger, axis=on_dim), (lax.axis_index(group_axis...]
  transfers between devices with their start and end apart: 3 -> 9, of which waited for: 2 -> 8; matrix products, arithmetic and copies ran while one was open for 5% -> 1% of each run, Pallas kernels for 0% -> 0%
where the time goes in v1:
time: 455 us
  waiting for transfers between devices  327 us (72%)
  local copies, waits for them, and re-layouts  49.8 us (11%)
  matrix products  32.1 us (7%)
  other arithmetic  17.1 us (4%)
  blocking collectives  13.5 us (3%)
  between operations  13.5 us (3%)
    ppermute x7, waiting for transfers between devices, match_the_spots(): clean = lax.ppermute(clean, axis_name=group_axis, perm=state_next)  185 us
    reduce_scatter x1, waiting for transfers between devices, shards(): lax.psum_scatter(partial_sum, 'tm', scatter_dimension=2, tiled=True)  142 us
    unnamed x40, local copies, waits for them, and re-layouts  40.4 us
    dot_general x4, matrix products, shards(): lax.dot_general(centered, extended[lag:lag + rows], (((0,), (0,)), ((), (...  32.1 us
    psum x1, blocking collectives, shards(): total = lax.psum(jnp.sum(trajectory, axis=0), 'tm')  13.5 us
  transfers between devices with their start and end apart: 9, of which 8 were waited for; matrix products, arithmetic and copies ran while one was open for 1% of the time, Pallas kernels for 0%

profile of v1, /device:TPU:0, one launch (start us, length us, event | category | flops | bytes accessed | tf_op | source)
XLA Modules:
  0.0 454.5 jit_solution(10431549818519657696)
XLA Ops:
  6.5 2.7 reduce_sum.9
  9.3 13.5 %psum.7 = f32[256]{0:T(256)S(1)} all-reduce(f32[256]{0:T(256)S(1)} %reduce_sum.9), channel_id=1, replica_groups=mesh['tm'=4,'feat'=8] {'tm'}, use_global_device_ids=true, to_apply=%region_1.0 | all-reduce | flops 256 | bytes 2048 | tf_op jit(solution)/shard_map/psum | solution.py:38
  22.8 2.5 subtract_convert_fusion
  25.4 26.3 %collective-permute-done = bf16[4096,256]{1,0:T(8,128)(2,1)S(1)} collective-permute-done((bf16[4096,256]{1,0:T(8,128)(2,1)S(1)}, bf16[4096,256]{1,0:T(8,128)(2,1)S(1)}, u32[]{:S(2)}, u32[]{:S(2)}) %collective-permute-start) | collective-permute-done | bytes 2097184 | tf_op jit(solution)/shard_map/ppermute | solution.py:17
  53.1 26.4 %collective-permute-done.1 = bf16[4096,256]{1,0:T(8,128)(2,1)S(1)} collective-permute-done((bf16[4096,256]{1,0:T(8,128)(2,1)S(1)}, bf16[4096,256]{1,0:T(8,128)(2,1)S(1)}, u32[]{:S(2)}, u32[]{:S(2)}) %collective-permute-start.1) | collective-permute-done | bytes 2097184 | tf_op jit(solution)/shard_map/ppermute | solution.py:17
  80.8 26.4 %collective-permute-done.2 = bf16[4096,256]{1,0:T(8,128)(2,1)S(1)} collective-permute-done((bf16[4096,256]{1,0:T(8,128)(2,1)S(1)}, bf16[4096,256]{1,0:T(8,128)(2,1)S(1)}, u32[]{:S(2)}, u32[]{:S(2)}) %collective-permute-start.2) | collective-permute-done | bytes 2097184 | tf_op jit(solution)/shard_map/ppermute | solution.py:17
  108.5 26.4 %collective-permute-done.3 = bf16[4096,256]{1,0:T(8,128)(2,1)S(1)} collective-permute-done((bf16[4096,256]{1,0:T(8,128)(2,1)S(1)}, bf16[4096,256]{1,0:T(8,128)(2,1)S(1)}, u32[]{:S(2)}, u32[]{:S(2)}) %collective-permute-start.3) | collective-permute-done | bytes 2097184 | tf_op jit(solution)/shard_map/ppermute | solution.py:17
  136.1 26.4 %collective-permute-done.4 = bf16[4096,256]{1,0:T(8,128)(2,1)S(1)} collective-permute-done((bf16[4096,256]{1,0:T(8,128)(2,1)S(1)}, bf16[4096,256]{1,0:T(8,128)(2,1)S(1)}, u32[]{:S(2)}, u32[]{:S(2)}) %collective-permute-start.4) | collective-permute-done | bytes 2097184 | tf_op jit(solution)/shard_map/ppermute | solution.py:17
  163.8 26.5 %collective-permute-done.5 = bf16[4096,256]{1,0:T(8,128)(2,1)} collective-permute-done((bf16[4096,256]{1,0:T(8,128)(2,1)S(1)}, bf16[4096,256]{1,0:T(8,128)(2,1)}, u32[]{:S(2)}, u32[]{:S(2)}) %collective-permute-start.5) | collective-permute-done | bytes 2097184 | tf_op jit(solution)/shard_map/ppermute | solution.py:17
  190.3 26.6 %collective-permute-done.6 = bf16[4096,256]{1,0:T(8,128)(2,1)} collective-permute-done((bf16[4096,256]{1,0:T(8,128)(2,1)}, bf16[4096,256]{1,0:T(8,128)(2,1)}, u32[]{:S(2)}, u32[]{:S(2)}) %collective-permute-start.6) | collective-permute-done | bytes 2097184 | tf_op jit(solution)/shard_map/ppermute | solution.py:17
  217.0 3.1 constant_dynamic-update-slice_fusion.15
  220.0 3.1 constant_dynamic-update-slice_fusion.14
  223.1 3.1 constant_dynamic-update-slice_fusion.13
  226.2 3.2 constant_dynamic-update-slice_fusion.12
  229.5 1.5 constant_dynamic-update-slice_fusion.11
  233.9 1.7 constant_dynamic-update-slice_fusion.8
  235.6 3.1 constant_dynamic-update-slice_fusion.7
  238.7 3.1 constant_dynamic-update-slice_fusion.6
  241.7 1.5 constant_dynamic-update-slice_fusion.5
  243.2 1.5 constant_dynamic-update-slice_fusion.4
  246.2 1.5 constant_dynamic-update-slice_fusion.2
  247.7 1.5 constant_dynamic-update-slice_fusion.1
  249.2 1.8 constant_dynamic-update-slice_fusion
  250.9 8.5 %constant_dynamic-slice_fusion.1 = bf16[4096,2048]{1,0:T(8,128)(2,1)S(1)} fusion(bf16[4096,4096]{1,0:T(8,128)(2,1)} %constant_dynamic-update-slice_fusion, s32[]{:T(128)S(6)} %select_n.14), kind=kLoop, calls=%fused_computation.35 | loop fusion | bytes 33554436 | tf_op jit(solution)/shard_map/jit(_roll_dynamic)/dynamic_slice | solution.py:19
  261.8 3.3 copy-done
  265.1 4.5 convolution_bitcast_fusion
  269.7 9.2 %fusion.13 = f32[1,256,2048]{2,1,0:T(8,128)S(1)} fusion(bf16[4096,256]{1,0:T(8,128)(2,1)S(1)} %subtract_convert_fusion, bf16[16,2048]{1,0:T(8,128)(2,1)S(1)} %collective-permute-done.7, bf16[4096,2048]{1,0:T(8,128)(2,1)} %copy-done), kind=kOutput, calls=%fused_computation.14 | convolution fusion | flops 4328521728 | bytes 21037056 | tf_op jit(solution)/shard_map/dot_general | solution.py:45
  278.9 9.2 %fusion.10 = f32[1,256,2048]{2,1,0:T(8,128)S(1)} fusion(bf16[4096,256]{1,0:T(8,128)(2,1)S(1)} %subtract_convert_fusion, bf16[16,2048]{1,0:T(8,128)(2,1)S(1)} %collective-permute-done.7, bf16[4096,2048]{1,0:T(8,128)(2,1)} %copy-done), kind=kOutput, calls=%fused_computation.13 | convolution fusion | flops 4328521728 | bytes 21037056 | tf_op jit(solution)/shard_map/dot_general | solution.py:45
  288.2 9.1 %fusion.16 = f32[1,256,2048]{2,1,0:T(8,128)} fusion(bf16[4096,256]{1,0:T(8,128)(2,1)S(1)} %subtract_convert_fusion, bf16[16,2048]{1,0:T(8,128)(2,1)S(1)} %collective-permute-done.7, bf16[4096,2048]{1,0:T(8,128)(2,1)} %copy-done), kind=kOutput, calls=%fused_computation.15 | convolution fusion | flops 4328521728 | bytes 21037056 | tf_op jit(solution)/shard_map/dot_general | solution.py:45
  297.3 5.0 %pad_maximum_fusion.2 = f32[4,256,2048]{2,1,0:T(8,128)} fusion(f32[1,256,2048]{2,1,0:T(8,128)} %fusion.16, f32[1,256,2048]{2,1,0:T(8,128)S(1)} %fusion.10, f32[1,256,2048]{2,1,0:T(8,128)S(1)} %fusion.13, f32[1,256,2048]{2,1,0:T(8,128)S(1)} %convolution_bitcast_fusion), kind=kLoop, calls=%fused_computation.11 | loop fusion | flops 6291456 | bytes 16777216 | tf_op jit(solution)/shard_map/stack | solution.py:53
  302.3 142.1 %reduce-scatter.2.cloned.1.call-done = f32[4,256,512]{2,1,0:T(8,128)} async-done(((f32[4,256,2048]{2,1,0:T(8,128)}), f32[4,256,512]{2,1,0:T(8,128)}) %reduce-scatter.2.cloned.1.call-update) | async-done | bytes 2097168 | tf_op jit(solution)/shard_map/reduce_scatter | solution.py:54
  444.4 3.3 broadcast_multiply_fusion
  (41 shorter events, 13.5 us)
Async XLA Ops:
  6.5 437.8 %reduce-scatter.2.cloned.1.call-start = ((), (), s32[]{:S(2)}) async-start(), calls=%async_computation.1 | async-start | bytes 10485760 | tf_op jit(solution)/shard_map/reduce_scatter | solution.py:54
  25.3 26.4 %collective-permute-start = (bf16[4096,256]{1,0:T(8,128)(2,1)S(1)}, bf16[4096,256]{1,0:T(8,128)(2,1)S(1)}, u32[]{:S(2)}, u32[]{:S(2)}) collective-permute-start(bf16[4096,256]{1,0:T(8,128)(2,1)S(1)} %subtract_convert_fusion), channel_id=1, source_target_pairs={{0,1},{1,2},{2,3},{3,4},{4,5},{5,6},{6,7},{7,0},{8,9},{9,10},{10,1... | collective-permute-start | bytes 6291464 | tf_op jit(solution)/shard_map/ppermute | solution.py:17
  51.7 1.3 copy-start.2
  53.1 26.4 %collective-permute-start.1 = (bf16[4096,256]{1,0:T(8,128)(2,1)S(1)}, bf16[4096,256]{1,0:T(8,128)(2,1)S(1)}, u32[]{:S(2)}, u32[]{:S(2)}) collective-permute-start(bf16[4096,256]{1,0:T(8,128)(2,1)S(1)} %collective-permute-done), channel_id=1, source_target_pairs={{0,1},{1,2},{2,3},{3,4},{4,5},{5,6},{6,7},{7,0},{8,9},{9,10},{10,1... | collective-permute-start | bytes 6291464 | tf_op jit(solution)/shard_map/ppermute | solution.py:17
  79.4 1.4 copy-start.4
  80.8 26.4 %collective-permute-start.2 = (bf16[4096,256]{1,0:T(8,128)(2,1)S(1)}, bf16[4096,256]{1,0:T(8,128)(2,1)S(1)}, u32[]{:S(2)}, u32[]{:S(2)}) collective-permute-start(bf16[4096,256]{1,0:T(8,128)(2,1)S(1)} %collective-permute-done.1), channel_id=1, source_target_pairs={{0,1},{1,2},{2,3},{3,4},{4,5},{5,6},{6,7},{7,0},{8,9},{9,10},{10,1... | collective-permute-start | bytes 6291464 | tf_op jit(solution)/shard_map/ppermute | solution.py:17
  107.2 1.3 copy-start.6
  108.5 26.4 %collective-permute-start.3 = (bf16[4096,256]{1,0:T(8,128)(2,1)S(1)}, bf16[4096,256]{1,0:T(8,128)(2,1)S(1)}, u32[]{:S(2)}, u32[]{:S(2)}) collective-permute-start(bf16[4096,256]{1,0:T(8,128)(2,1)S(1)} %collective-permute-done.2), channel_id=1, source_target_pairs={{0,1},{1,2},{2,3},{3,4},{4,5},{5,6},{6,7},{7,0},{8,9},{9,10},{10,1... | collective-permute-start | bytes 6291464 | tf_op jit(solution)/shard_map/ppermute | solution.py:17
  134.8 1.3 copy-start.8
  136.1 26.4 %collective-permute-start.4 = (bf16[4096,256]{1,0:T(8,128)(2,1)S(1)}, bf16[4096,256]{1,0:T(8,128)(2,1)S(1)}, u32[]{:S(2)}, u32[]{:S(2)}) collective-permute-start(bf16[4096,256]{1,0:T(8,128)(2,1)S(1)} %collective-permute-done.3), channel_id=1, source_target_pairs={{0,1},{1,2},{2,3},{3,4},{4,5},{5,6},{6,7},{7,0},{8,9},{9,10},{10,1... | collective-permute-start | bytes 6291464 | tf_op jit(solution)/shard_map/ppermute | solution.py:17
  162.5 1.3 copy-start.10
  163.8 26.5 %collective-permute-start.5 = (bf16[4096,256]{1,0:T(8,128)(2,1)S(1)}, bf16[4096,256]{1,0:T(8,128)(2,1)}, u32[]{:S(2)}, u32[]{:S(2)}) collective-permute-start(bf16[4096,256]{1,0:T(8,128)(2,1)S(1)} %collective-permute-done.4), channel_id=1, source_target_pairs={{0,1},{1,2},{2,3},{3,4},{4,5},{5,6},{6,7},{7,0},{8,9},{9,10},{10,1... | collective-permute-start | bytes 6291464 | tf_op jit(solution)/shard_map/ppermute | solution.py:17
  190.3 26.7 %collective-permute-start.6 = (bf16[4096,256]{1,0:T(8,128)(2,1)}, bf16[4096,256]{1,0:T(8,128)(2,1)}, u32[]{:S(2)}, u32[]{:S(2)}) collective-permute-start(bf16[4096,256]{1,0:T(8,128)(2,1)} %collective-permute-done.5), channel_id=1, source_target_pairs={{0,1},{1,2},{2,3},{3,4},{4,5},{5,6},{6,7},{7,0},{8,9},{9,10},{10,1... | collective-permute-start | bytes 6291464 | tf_op jit(solution)/shard_map/ppermute | solution.py:17
  190.3 39.2 %copy-start.7 = (bf16[4096,256]{1,0:T(8,128)(2,1)S(1)}, bf16[4096,256]{1,0:T(8,128)(2,1)}, u32[]{:S(2)}) copy-start(bf16[4096,256]{1,0:T(8,128)(2,1)} %copy-done.6) | copy-start | bytes 6291460
  190.3 40.7 %copy-start.5 = (bf16[4096,256]{1,0:T(8,128)(2,1)S(1)}, bf16[4096,256]{1,0:T(8,128)(2,1)}, u32[]{:S(2)}) copy-start(bf16[4096,256]{1,0:T(8,128)(2,1)} %copy-done.4) | copy-start | bytes 6291460
  190.3 42.1 %copy-start.3 = (bf16[4096,256]{1,0:T(8,128)(2,1)S(1)}, bf16[4096,256]{1,0:T(8,128)(2,1)}, u32[]{:S(2)}) copy-start(bf16[4096,256]{1,0:T(8,128)(2,1)} %copy-done.2) | copy-start | bytes 6291460
  190.3 43.6 %copy-start.1 = (f32[4096,256]{1,0:T(8,128)S(1)}, f32[4096,256]{1,0:T(8,128)}, u32[]{:S(2)}) copy-start(f32[4096,256]{1,0:T(8,128)} %param.2) | copy-start | bytes 12582916
  226.2 15.5 %copy-start.11 = (bf16[4096,256]{1,0:T(8,128)(2,1)S(1)}, bf16[4096,256]{1,0:T(8,128)(2,1)}, u32[]{:S(2)}) copy-start(bf16[4096,256]{1,0:T(8,128)(2,1)} %copy-done.10) | copy-start | bytes 6291460
  229.5 13.8 %copy-start.9 = (bf16[4096,256]{1,0:T(8,128)(2,1)S(1)}, bf16[4096,256]{1,0:T(8,128)(2,1)}, u32[]{:S(2)}) copy-start(bf16[4096,256]{1,0:T(8,128)(2,1)} %copy-done.8) | copy-start | bytes 6291460
  259.4 5.7 %copy-start = (bf16[4096,2048]{1,0:T(8,128)(2,1)}, bf16[4096,2048]{1,0:T(8,128)(2,1)S(1)}, u32[]{:S(2)}) copy-start(bf16[4096,2048]{1,0:T(8,128)(2,1)S(1)} %constant_dynamic-slice_fusion.1) | copy-start | bytes 50331652
  260.4 9.3 %collective-permute-start.7 = (bf16[16,2048]{1,0:T(8,128)(2,1)S(1)}, bf16[16,2048]{1,0:T(8,128)(2,1)S(1)}, u32[]{:S(2)}, u32[]{:S(2)}) collective-permute-start(bf16[16,2048]{1,0:T(8,128)(2,1)S(1)} %constant_dynamic-slice_fusion), channel_id=1, source_target_pairs={{8,0},{16,8},{24,16},{9,1},{17,9},{25,17},{10,2},{18,10},{26,18},{... | collective-permute-start | bytes 196616 | tf_op jit(solution)/shard_map/ppermute | solution.py:32
  297.3 147.1 %copy-start.12 = (f32[4]{0:T(128)S(1)}, f32[4]{0:T(128)}, u32[]{:S(2)}) copy-start(f32[4]{0:T(128)} %constant.43) | copy-start | bytes 52
Sparse Core Ops, SparseCore 0:
  302.4 141.8 reduce-scatter.1
